TPU v7x, 32 devices: a whole 2x2x4 slice. The times are simulated.
32 devices in a mesh: dp: 16 (over z, y, x), mp: 2 (over core).
Axes of the slice: x: 2, y: 2, z: 4, core: 2. Of those that a mesh axis runs over, the one named last changes fastest.
Arguments:
- tokens: bfloat16 [32768, 768], P('dp'), may hold values from -6 to 6
- segments: int32 [32768], P('dp'), may hold values from 0 to 32, as said below
- sentence_dest: int32 [2048, 2], P('dp'), may hold values from 0 to 15, as said below
- pair_source: int32 [2048, 2], P('dp'), may hold values from 0 to 15, as said below
- labels: int32 [1024], P('dp'), may hold values from 0 to 5
- params: float32 [2, 3541248], P('mp', 'dp'), as said below
- first: float32 [2, 3541248], P('mp', 'dp')
- second: float32 [2, 3541248], P('mp', 'dp'), as said below
- shared: float32 [6, 768], replicated, as said below
- shared_first: float32 [6, 768], replicated
- shared_second: float32 [6, 768], replicated, as said below
Outputs:
- encoded: bfloat16 [32768, 768], P('dp')
- input_grad: float32 [32768, 768], P('dp')
- grad_norm: float32 [1], replicated
- params_new: float32 [2, 3541248], P('mp', 'dp')
- first_new: float32 [2, 3541248], P('mp', 'dp')
- second_new: float32 [2, 3541248], P('mp', 'dp')
- params_low: bfloat16 [2, 3541248], P('mp', 'dp')
- shared_new: float32 [6, 768], replicated
- shared_first_new: float32 [6, 768], replicated
- shared_second_new: float32 [6, 768], replicated
- params_grad: float32 [2, 3541248], P('mp', 'dp')
- shared_grad: float32 [6, 768], replicated
Inputs may be any that keep to these rules, and one draw needn't show every extreme that they name: `segments`: within each row of 512 positions ids never fall; each id 0 to 31 covers 1 to 16 positions and slot 0 exactly 16; id 32 marks the padding at a row's end. `sentence_dest`: column 0 is the scoring device, column 1 the place 0 to 7 among the sentences that this device sends there; each device sends exactly 8 or none of its sentences to each device, and each (device, place) occurs once per sender. `pair_source`: column 0 is the sending device, column 1 the place; each names a sentence whose sentence_dest points to this device and place, every sentence exactly once; items 2j and 2j+1 form pair j. `params`: laid out as the steps say. `second`: Positive. `shared`: Rows: first gain, first bias, second gain, second bias, attention output bias, feed-forward output bias. `shared_second`: Positive.
All inputs are finite; a program needn't handle non-finite values.
Results may differ from a plain program's by a relative error of at most 0.018.
Values may be sent and summed in bfloat16 or wider, within the bound.
A program may use at most 256 MiB of HBM per device.

v0:
```python
from functools import partial
import math

import jax
import jax.numpy as jnp
from jax import lax
from jax.sharding import PartitionSpec as P

HEAD_DIM = 64
FF = 3072
ROW = 512
SEG = 32
RPM = 2
MB = 2


LOSS_SCALE = 1024.0
CLIP_NORM = 0.5
LEARN_RATE = 0.1
SHARED_RATE = 0.5
BETA_ONE = 0.9
BETA_TWO = 0.999
ADAM_EPS = 1e-08
DECAY = 0.01
NORM_EPS = 1e-12
STEP_COUNT = 10.0
TOP_PRECISION = lax.Precision.HIGHEST


def normalize(values_in, scale_vec, shift_vec):
    center = jnp.mean(values_in, -1, keepdims=True)
    centered = values_in - center
    spread = jnp.mean(centered * centered, -1, keepdims=True)
    return centered * lax.rsqrt(spread + NORM_EPS) * scale_vec + shift_vec


def unpack(packed, features, head_cols, ffn_cols):
    pieces = []
    offset = 0
    for height, extent in (
        (features, 3 * head_cols),
        (head_cols, features),
        (features, ffn_cols),
        (ffn_cols, features),
    ):
        pieces.append(packed[offset : offset + height * extent].reshape(height, extent))
        offset = offset + height * extent
    for extent in (head_cols, head_cols, ffn_cols):
        pieces.append(packed[offset : offset + extent])
        offset = offset + extent
    return pieces


def pair_loss(pair_items, labels):
    first_vec = pair_items[..., 0::2, :]
    second_vec = pair_items[..., 1::2, :]
    inner_prod = jnp.sum(first_vec * second_vec, -1)
    cosine = (
        inner_prod
        * lax.rsqrt(jnp.sum(first_vec * first_vec, -1) + 1e-06)
        * lax.rsqrt(jnp.sum(second_vec * second_vec, -1) + 1e-06)
    )
    error_term = cosine - labels.astype(jnp.float32) / 5.0
    return LOSS_SCALE * jnp.sum(error_term * error_term)


def adamw(weight, moment_one, moment_two, gradient, factor, step_count, rate):
    clipped = gradient * factor
    first_new = BETA_ONE * moment_one + (1.0 - BETA_ONE) * clipped
    second_new = BETA_TWO * moment_two + (1.0 - BETA_TWO) * clipped * clipped
    first_hat = first_new / (1.0 - BETA_ONE**step_count)
    second_hat = second_new / (1.0 - BETA_TWO**step_count)
    weight_new = weight - rate * (first_hat / (jnp.sqrt(second_hat) + ADAM_EPS) + DECAY * weight)
    return (weight_new, first_new, second_new)


def per_device(
    tokens,
    segments,
    sentence_dest,
    pair_source,
    labels,
    params,
    first,
    second,
    shared,
    shared_first,
    shared_second,
):
    features = tokens.shape[1]
    head_cols = features // lax.axis_size("mp")
    ffn_cols = FF // lax.axis_size("mp")
    heads_dev = head_cols // HEAD_DIM
    dp_count = lax.axis_size("dp")
    sent_slots = MB * RPM * SEG
    slot_capacity = max(2, sent_slots // dp_count)
    score_scale = HEAD_DIM ** (-0.5)
    flat_rows = RPM * ROW
    params_total = lax.axis_size("mp") * params.shape[1] * dp_count + 6 * features
    low_shard = params.astype(jnp.bfloat16)

    def weights_now():
        return unpack(
            lax.all_gather(low_shard, "dp", axis=1, tiled=True)[0], features, head_cols, ffn_cols
        )

    slot_ids = jnp.arange(SEG, dtype=jnp.int32)

    def pooling_matrix(block_segments):
        onehot = (block_segments[:, None, :] == slot_ids[None, :, None]).astype(jnp.float32)
        return onehot / jnp.sum(onehot, 2, keepdims=True)

    def masked_scores(queries, keys_low, block_segments):
        same_doc = (block_segments[:, :, None] == block_segments[:, None, :])[:, None]
        scores = (
            jnp.einsum("rqhd,rkhd->rhqk", queries, keys_low, preferred_element_type=jnp.float32)
            * score_scale
        )
        return jnp.where(same_doc, scores, -1e30)

    def forward_step(carried, inputs):
        tokens_block, block_segments = inputs
        w_qkv, w_attn, w_in, w_out, b_query, b_value, b_in = weights_now()
        tokens_flat = tokens_block.reshape(flat_rows, features)
        projected = jnp.dot(tokens_flat, w_qkv, preferred_element_type=jnp.float32)
        queries = (
            (projected[:, :head_cols] + b_query)
            .astype(jnp.bfloat16)
            .reshape(RPM, ROW, heads_dev, HEAD_DIM)
        )
        keys_low = (
            projected[:, head_cols : 2 * head_cols]
            .astype(jnp.bfloat16)
            .reshape(RPM, ROW, heads_dev, HEAD_DIM)
        )
        values_low = (
            (projected[:, 2 * head_cols :] + b_value)
            .astype(jnp.bfloat16)
            .reshape(RPM, ROW, heads_dev, HEAD_DIM)
        )
        scores = masked_scores(queries, keys_low, block_segments)
        row_max = jnp.max(scores, -1, keepdims=True)
        exponent = jnp.exp(scores - row_max)
        row_total = jnp.sum(exponent, -1, keepdims=True)
        attn_probs = (exponent / row_total).astype(jnp.bfloat16)
        log_total = row_max + jnp.log(row_total)
        mixed_heads = jnp.einsum(
            "rhqk,rkhd->rqhd", attn_probs, values_low, preferred_element_type=jnp.float32
        )
        mixed_heads = mixed_heads.reshape(flat_rows, head_cols).astype(jnp.bfloat16)
        attn_term = jnp.dot(mixed_heads, w_attn, preferred_element_type=jnp.float32)
        attn_out = lax.psum(attn_term.astype(jnp.bfloat16), "mp").astype(jnp.float32) + shared[4]
        resid_one = tokens_flat.astype(jnp.float32) + attn_out
        hidden = normalize(resid_one, shared[0], shared[1])
        up_proj = (
            jnp.dot(hidden.astype(jnp.bfloat16), w_in, preferred_element_type=jnp.float32) + b_in
        )
        activated = jax.nn.gelu(up_proj, approximate=False).astype(jnp.bfloat16)
        ffn_term = jnp.dot(activated, w_out, preferred_element_type=jnp.float32)
        ffn_out = lax.psum(ffn_term.astype(jnp.bfloat16), "mp").astype(jnp.float32) + shared[5]
        resid_two = hidden + ffn_out
        encoded_flat = normalize(resid_two, shared[2], shared[3])
        block_encodings = encoded_flat.reshape(RPM, ROW, features)
        pooled = jnp.einsum(
            "kvf,kfo->kvo", pooling_matrix(block_segments), block_encodings, precision=TOP_PRECISION
        ).astype(jnp.bfloat16)
        saved_state = (
            queries,
            keys_low,
            values_low,
            log_total,
            mixed_heads,
            resid_one,
            up_proj,
            activated,
            resid_two,
        )
        return (carried, (block_encodings.astype(jnp.bfloat16), pooled, saved_state))

    token_blocks = tokens.reshape(MB, RPM, ROW, features)
    segment_blocks = segments.reshape(MB, RPM, ROW)
    ignored, (encoded, pooled_all, saved_all) = lax.scan(
        forward_step, jnp.zeros((), jnp.float32), (token_blocks, segment_blocks)
    )
    pooled_flat = pooled_all.reshape(sent_slots, features)
    code_ids = jnp.arange(dp_count * slot_capacity, dtype=jnp.int32)
    send_code = sentence_dest[:, 0] * slot_capacity + sentence_dest[:, 1]
    send_map = (code_ids[:, None] == send_code[None, :]).astype(jnp.bfloat16)
    outgoing = jnp.dot(send_map, pooled_flat, preferred_element_type=jnp.float32).astype(
        jnp.bfloat16
    )
    outgoing = outgoing.reshape(dp_count, slot_capacity, features)
    incoming = lax.all_to_all(outgoing, "dp", split_axis=0, concat_axis=0, tiled=True).reshape(
        dp_count * slot_capacity, features
    )
    take_code = pair_source[:, 0] * slot_capacity + pair_source[:, 1]
    take_map = (take_code[:, None] == code_ids[None, :]).astype(jnp.bfloat16)
    pair_items = jnp.dot(take_map, incoming, preferred_element_type=jnp.float32)
    item_grad = jax.grad(pair_loss)(pair_items, labels).astype(jnp.bfloat16)
    returning = jnp.dot(take_map.T, item_grad, preferred_element_type=jnp.float32).astype(
        jnp.bfloat16
    )
    returning = returning.reshape(dp_count, slot_capacity, features)
    arrived = lax.all_to_all(returning, "dp", split_axis=0, concat_axis=0, tiled=True).reshape(
        dp_count * slot_capacity, features
    )
    pooled_grad = jnp.dot(send_map.T, arrived, preferred_element_type=jnp.float32).reshape(
        MB, RPM, SEG, features
    )

    def backward_step(carried, inputs):
        shared_acc, flat_acc = carried
        tokens_block, block_segments, sentence_gradient, saved_state = inputs
        (
            queries,
            keys_low,
            values_low,
            log_total,
            mixed_heads,
            resid_one,
            up_proj,
            activated,
            resid_two,
        ) = saved_state
        w_qkv, w_attn, w_in, w_out, b_query, b_value, b_in = weights_now()
        tokens_flat = tokens_block.reshape(flat_rows, features)
        encoded_grad = jnp.einsum(
            "jix,jip->jxp",
            pooling_matrix(block_segments),
            sentence_gradient,
            precision=TOP_PRECISION,
        ).reshape(flat_rows, features)
        ignored_two, norm_two_back = jax.vjp(normalize, resid_two, shared[2], shared[3])
        resid_two_grad, scale_two, shift_two = norm_two_back(encoded_grad)
        ffn_grad = resid_two_grad.astype(jnp.bfloat16)
        ignored_act, gelu_back = jax.vjp(partial(jax.nn.gelu, approximate=False), up_proj)
        act_grad = jnp.dot(ffn_grad, w_out.T, preferred_element_type=jnp.float32)
        up_grad = gelu_back(act_grad)[0].astype(jnp.bfloat16)
        hidden, norm_one_back = jax.vjp(normalize, resid_one, shared[0], shared[1])
        w_out_grad = jnp.dot(activated.T, ffn_grad, preferred_element_type=jnp.float32)
        w_in_grad = jnp.dot(
            hidden.astype(jnp.bfloat16).T, up_grad, preferred_element_type=jnp.float32
        )
        hidden_term = jnp.dot(up_grad, w_in.T, preferred_element_type=jnp.float32)
        hidden_grad = resid_two_grad + lax.psum(hidden_term.astype(jnp.bfloat16), "mp").astype(
            jnp.float32
        )
        resid_one_grad, scale_one, shift_one = norm_one_back(hidden_grad)
        attn_grad = resid_one_grad.astype(jnp.bfloat16)
        w_attn_grad = jnp.dot(mixed_heads.T, attn_grad, preferred_element_type=jnp.float32)
        mixed_grad = jnp.dot(attn_grad, w_attn.T, preferred_element_type=jnp.float32)
        mixed_grad = mixed_grad.astype(jnp.bfloat16).reshape(RPM, ROW, heads_dev, HEAD_DIM)
        attn_probs = jnp.exp(masked_scores(queries, keys_low, block_segments) - log_total)
        value_grad = jnp.einsum(
            "rhqk,rqhd->rkhd",
            attn_probs.astype(jnp.bfloat16),
            mixed_grad,
            preferred_element_type=jnp.float32,
        )
        prob_grad = jnp.einsum(
            "rqhd,rkhd->rhqk", mixed_grad, values_low, preferred_element_type=jnp.float32
        )
        row_inner = jnp.sum(prob_grad * attn_probs, -1, keepdims=True)
        score_grad = (attn_probs * (prob_grad - row_inner)).astype(jnp.bfloat16)
        query_grad = (
            jnp.einsum("rhqk,rkhd->rqhd", score_grad, keys_low, preferred_element_type=jnp.float32)
            * score_scale
        )
        key_grad = (
            jnp.einsum("rhqk,rqhd->rkhd", score_grad, queries, preferred_element_type=jnp.float32)
            * score_scale
        )
        query_key_value_gradient = jnp.concatenate(
            [
                query_grad.reshape(flat_rows, head_cols),
                key_grad.reshape(flat_rows, head_cols),
                value_grad.reshape(flat_rows, head_cols),
            ],
            1,
        ).astype(jnp.bfloat16)
        w_qkv_grad = jnp.dot(
            tokens_flat.T, query_key_value_gradient, preferred_element_type=jnp.float32
        )
        input_term = jnp.dot(query_key_value_gradient, w_qkv.T, preferred_element_type=jnp.float32)
        input_grad = resid_one_grad + lax.psum(input_term.astype(jnp.bfloat16), "mp").astype(
            jnp.float32
        )
        column_sums = jnp.sum(query_key_value_gradient.astype(jnp.float32), 0)
        grad_flat = jnp.concatenate(
            [
                w_qkv_grad.reshape(-1),
                w_attn_grad.reshape(-1),
                w_in_grad.reshape(-1),
                w_out_grad.reshape(-1),
                column_sums[:head_cols],
                column_sums[2 * head_cols :],
                jnp.sum(up_grad.astype(jnp.float32), 0),
            ]
        )[None]
        shared_step = jnp.stack(
            [
                scale_one,
                shift_one,
                scale_two,
                shift_two,
                jnp.sum(attn_grad.astype(jnp.float32), 0),
                jnp.sum(ffn_grad.astype(jnp.float32), 0),
            ]
        )
        flat_acc = flat_acc + lax.psum_scatter(grad_flat, "dp", scatter_dimension=1, tiled=True)
        return ((shared_acc + shared_step, flat_acc), input_grad)

    flat_start = jnp.zeros((1, params.shape[1]), jnp.float32)
    (shared_acc, flat_acc), input_grads = lax.scan(
        backward_step,
        (jnp.zeros_like(shared), flat_start),
        (token_blocks, segment_blocks, pooled_grad, saved_all),
    )
    flat_grad = flat_acc
    flat_grad = flat_grad / LOSS_SCALE
    local_squares = jnp.sum(flat_grad * flat_grad)
    shared_total = lax.psum(shared_acc, "dp")
    total_squares = lax.psum(local_squares, ("dp", "mp"))
    shared_grad = shared_total / LOSS_SCALE
    norm_value = jnp.sqrt(total_squares + jnp.sum(shared_grad * shared_grad))
    factor = jnp.minimum(1.0, CLIP_NORM / norm_value)
    step_count = STEP_COUNT
    params_new, first_new, second_new = adamw(
        params, first, second, flat_grad, factor, step_count, LEARN_RATE
    )
    shared_new, shared_first_new, shared_second_new = adamw(
        shared, shared_first, shared_second, shared_grad, factor, step_count, SHARED_RATE
    )
    grad_unit = math.sqrt(params_total) / CLIP_NORM
    params_grad = flat_grad * factor * grad_unit
    shared_grad_out = shared_grad * factor * grad_unit
    return (
        encoded.reshape(MB * RPM * ROW, features),
        input_grads.reshape(MB * RPM * ROW, features),
        norm_value.reshape(1),
        params_new,
        first_new,
        second_new,
        params_new.astype(jnp.bfloat16),
        shared_new,
        shared_first_new,
        shared_second_new,
        params_grad,
        shared_grad_out,
    )


def solution(mesh):
    in_specs = (
        P("dp", None),
        P("dp"),
        P("dp", None),
        P("dp", None),
        P("dp"),
        P("mp", "dp"),
        P("mp", "dp"),
        P("mp", "dp"),
        P(),
        P(),
        P(),
    )
    out_specs = (
        P("dp", None),
        P("dp", None),
        P(),
        P("mp", "dp"),
        P("mp", "dp"),
        P("mp", "dp"),
        P("mp", "dp"),
        P(),
        P(),
        P(),
        P("mp", "dp"),
        P(),
    )
    return jax.shard_map(
        per_device, mesh=mesh, in_specs=in_specs, out_specs=out_specs, check_vma=False
    )
```

profile of v0, /device:TPU:0, one launch (start us, length us, event | category | flops | bytes accessed | tf_op | source)
XLA Modules:
  0.0 3310.9 jit_solution(3628532116276965584)
XLA Ops:
  18.3 1072.0 %while.46 = (s32[]{:T(128)}, bf16[2,2,512,768]{3,2,1,0:T(8,128)(2,1)}, bf16[2,2,32,768]{3,2,1,0:T(8,128)(2,1)S(1)}, bf16[2,2,512,6,64]{2,1,4,3,0:T(2,128)(2,1)},...) while((s32[]{:T(128)}, ...), condition=%wide.region_10.11_spmd.clone, body=%wide.region_0.10_spmd.clone.sunk | while | flops 8542994944 | bytes 398459968 | solution.py:182
  43.5 228.5 %all-reduce.21.cloned.1.call-done = bf16[3541248]{0:T(1024)(128)(2,1)} async-done(((bf16[3541248]{0:T(1024)(128)(2,1)}), bf16[3541248]{0:T(1024)(128)(2,1)}) %all-reduce.21.cloned.1.call-update) | async-done | bytes 7082512 | tf_op jit(solution)/shard_map/while
  272.0 69.0 %reshape.574 = bf16[1,3541248]{1,0:T(2,128)(2,1)S(1)} reshape(bf16[3541248]{0:T(1024)(128)(2,1)} %all-reduce.21.cloned.1.call-done) | data formatting | bytes 14164992 | tf_op jit(solution)/shard_map/while
  351.7 35.6 %slice_reduce_fusion.27 = bf16[884736]{0:T(1024)(128)(2,1)} fusion(bf16[1,3541248]{1,0:T(2,128)(2,1)S(1)} %reshape.574), kind=kLoop, calls=%fused_computation.30.clone.1 | loop fusion | bytes 3538944 | tf_op jit(solution)/shard_map/while/body/eval_jaxpr/slice | solution.py:46
  429.7 53.2 %slice_reduce_fusion.26 = (bf16[1179648]{0:T(1024)(128)(2,1)}, bf16[1179648]{0:T(1024)(128)(2,1)}) fusion(bf16[1,3541248]{1,0:T(2,128)(2,1)} %copy-done.2), kind=kLoop, calls=%fused_computation.28.clone.1 | loop fusion | bytes 9437184 | tf_op jit(solution)/shard_map/while/body/eval_jaxpr/slice | solution.py:46
  579.2 227.0 %all-reduce.21.cloned.1.call-done = bf16[3541248]{0:T(1024)(128)(2,1)} async-done(((bf16[3541248]{0:T(1024)(128)(2,1)}), bf16[3541248]{0:T(1024)(128)(2,1)}) %all-reduce.21.cloned.1.call-update) | async-done | bytes 7082512 | tf_op jit(solution)/shard_map/while
  806.2 68.9 %reshape.574 = bf16[1,3541248]{1,0:T(2,128)(2,1)S(1)} reshape(bf16[3541248]{0:T(1024)(128)(2,1)} %all-reduce.21.cloned.1.call-done) | data formatting | bytes 14164992 | tf_op jit(solution)/shard_map/while
  885.8 35.6 %slice_reduce_fusion.27 = bf16[884736]{0:T(1024)(128)(2,1)} fusion(bf16[1,3541248]{1,0:T(2,128)(2,1)S(1)} %reshape.574), kind=kLoop, calls=%fused_computation.30.clone.1 | loop fusion | bytes 3538944 | tf_op jit(solution)/shard_map/while/body/eval_jaxpr/slice | solution.py:46
  963.8 53.2 %slice_reduce_fusion.26 = (bf16[1179648]{0:T(1024)(128)(2,1)}, bf16[1179648]{0:T(1024)(128)(2,1)}) fusion(bf16[1,3541248]{1,0:T(2,128)(2,1)} %copy-done.2), kind=kLoop, calls=%fused_computation.28.clone.1 | loop fusion | bytes 9437184 | tf_op jit(solution)/shard_map/while/body/eval_jaxpr/slice | solution.py:46
  1124.7 2047.9 %while.47 = (s32[]{:T(128)}, f32[6,768]{1,0:T(8,128)}, f32[1,221328]{1,0:T(1,128)}, f32[2,1024,768]{2,1,0:T(8,128)}, f32[2,1024,768]{2,1,0:T(8,128)}, /*index=5*...) while((s32[]{:T(128)}, f32[6,768]{1,0:T(8,128)}, ...), condition=%wide.region_36.37_spmd.clone, body=%wide.region_14.36_spmd.clone.sunk | while | flops 17043947520 | bytes 761370240 | solution.py:314
  1192.5 181.0 %all-reduce.27.cloned.1.call-done = bf16[3541248]{0:T(1024)(128)(2,1)} async-done(((bf16[3541248]{0:T(1024)(128)(2,1)}), bf16[3541248]{0:T(1024)(128)(2,1)}) %all-reduce.27.cloned.1.call-update) | async-done | bytes 7082512 | tf_op jit(solution)/shard_map/while
  1373.5 68.6 %reshape.582 = bf16[1,3541248]{1,0:T(2,128)(2,1)} reshape(bf16[3541248]{0:T(1024)(128)(2,1)} %all-reduce.27.cloned.1.call-done) | data formatting | bytes 14164992 | tf_op jit(solution)/shard_map/while
  1442.1 53.6 %slice_reduce_fusion.30 = (bf16[1179648]{0:T(1024)(128)(2,1)}, bf16[1179648]{0:T(1024)(128)(2,1)}) fusion(bf16[1,3541248]{1,0:T(2,128)(2,1)} %reshape.582), kind=kLoop, calls=%fused_computation.138.clone.1 | loop fusion | bytes 9437184 | tf_op jit(solution)/shard_map/while/body/eval_jaxpr/slice | solution.py:46
  1545.7 36.6 %slice_reduce_fusion.32 = bf16[884736]{0:T(1024)(128)(2,1)} fusion(bf16[1,3541248]{1,0:T(2,128)(2,1)} %reshape.582), kind=kLoop, calls=%fused_computation.141.clone.1 | loop fusion | bytes 3538944 | tf_op jit(solution)/shard_map/while/body/eval_jaxpr/slice | solution.py:46
  1691.6 54.1 %broadcast_in_dim.266 = f32[1,3541248]{1,0:T(1,128)} reshape(f32[3541248]{0:T(1024)} %constant_dynamic-update-slice_fusion.42) | data formatting | bytes 28329984 | tf_op jit(solution)/shard_map/while/body/eval_jaxpr/broadcast_in_dim | solution.py:289
  1750.8 391.5 %all-reduce.31.cloned.1.call-done = f32[1,3541248]{1,0:T(1,128)} async-done(((f32[1,3541248]{1,0:T(1,128)}), f32[1,3541248]{1,0:T(1,128)}) %all-reduce.31.cloned.1.call-update) | async-done | bytes 14165008 | tf_op jit(solution)/shard_map/while
  2213.9 182.4 %all-reduce.27.cloned.1.call-done = bf16[3541248]{0:T(1024)(128)(2,1)} async-done(((bf16[3541248]{0:T(1024)(128)(2,1)}), bf16[3541248]{0:T(1024)(128)(2,1)}) %all-reduce.27.cloned.1.call-update) | async-done | bytes 7082512 | tf_op jit(solution)/shard_map/while
  2396.3 68.6 %reshape.582 = bf16[1,3541248]{1,0:T(2,128)(2,1)} reshape(bf16[3541248]{0:T(1024)(128)(2,1)} %all-reduce.27.cloned.1.call-done) | data formatting | bytes 14164992 | tf_op jit(solution)/shard_map/while
  2464.9 53.3 %slice_reduce_fusion.30 = (bf16[1179648]{0:T(1024)(128)(2,1)}, bf16[1179648]{0:T(1024)(128)(2,1)}) fusion(bf16[1,3541248]{1,0:T(2,128)(2,1)} %reshape.582), kind=kLoop, calls=%fused_computation.138.clone.1 | loop fusion | bytes 9437184 | tf_op jit(solution)/shard_map/while/body/eval_jaxpr/slice | solution.py:46
  2568.4 36.6 %slice_reduce_fusion.32 = bf16[884736]{0:T(1024)(128)(2,1)} fusion(bf16[1,3541248]{1,0:T(2,128)(2,1)} %reshape.582), kind=kLoop, calls=%fused_computation.141.clone.1 | loop fusion | bytes 3538944 | tf_op jit(solution)/shard_map/while/body/eval_jaxpr/slice | solution.py:46
  2714.4 54.1 %broadcast_in_dim.266 = f32[1,3541248]{1,0:T(1,128)} reshape(f32[3541248]{0:T(1024)} %constant_dynamic-update-slice_fusion.42) | data formatting | bytes 28329984 | tf_op jit(solution)/shard_map/while/body/eval_jaxpr/broadcast_in_dim | solution.py:289
  2773.6 391.5 %all-reduce.31.cloned.1.call-done = f32[1,3541248]{1,0:T(1,128)} async-done(((f32[1,3541248]{1,0:T(1,128)}), f32[1,3541248]{1,0:T(1,128)}) %all-reduce.31.cloned.1.call-update) | async-done | bytes 14165008 | tf_op jit(solution)/shard_map/while
  3176.1 39.5 %psum.42 = f32[]{:T(128)} all-reduce(f32[]{:T(128)} %multiply_reduce_fusion.9), channel_id=1, replica_groups=mesh['dp'=16,'mp'=2] {'dp','mp'}, use_global_device_ids=true, to_apply=%region_38.39 | all-reduce | flops 1 | bytes 8 | tf_op jit(solution)/shard_map/psum | solution.py:323
  3215.6 75.8 %psum.43 = f32[6,768]{1,0:T(8,128)S(1)} all-reduce(f32[6,768]{1,0:T(8,128)} %get-tuple-element.221), channel_id=1, replica_groups=mesh['dp'=16,'mp'=2] {'dp'}, use_global_device_ids=true, to_apply=%region_39.40 | all-reduce | flops 4608 | bytes 36864 | tf_op jit(solution)/shard_map/psum | solution.py:322
  (573 shorter events, 822.9 us)
Async XLA Ops:
  18.3 1072.0 %copy-start.45 = (s32[128]{0:T(128)S(1)}, s32[128]{0:T(128)}, u32[]{:S(2)}) copy-start(s32[128]{0:T(128)} %add_bitcast_fusion.1) | copy-start | bytes 1540
  18.3 1079.7 %copy-start.50 = (s32[128,2]{0,1:T(2,128)S(1)}, s32[128,2]{0,1:T(2,128)}, u32[]{:S(2)}) copy-start(s32[128,2]{0,1:T(2,128)} %param.18) | copy-start | bytes 3076
  18.3 1089.5 %copy-start.46 = (s32[64]{0:T(128)S(1)}, s32[64]{0:T(128)}, u32[]{:S(2)}) copy-start(s32[64]{0:T(128)} %param.19) | copy-start | bytes 772
  18.5 253.5 %all-reduce.21.cloned.1.call-start = ((), (), s32[]{:S(2)}) async-start(), calls=%async_computation.2 | async-start | bytes 14168064 | tf_op jit(solution)/shard_map/while
  39.9 460.0 %all-reduce.23.cloned.1.call-start = ((), (), s32[]{:S(2)}) async-start(), calls=%async_computation.3 | async-start | bytes 3145728 | tf_op jit(solution)/shard_map/while/body/eval_jaxpr/psum | solution.py:152
  429.6 114.6 %all-reduce.25.cloned.1.call-start = ((), (), s32[]{:S(2)}) async-start(), calls=%async_computation.4 | async-start | bytes 3145728 | tf_op jit(solution)/shard_map/while/body/eval_jaxpr/psum | solution.py:160
  554.2 252.0 %all-reduce.21.cloned.1.call-start = ((), (), s32[]{:S(2)}) async-start(), calls=%async_computation.2 | async-start | bytes 14168064 | tf_op jit(solution)/shard_map/while
  575.6 458.4 %all-reduce.23.cloned.1.call-start = ((), (), s32[]{:S(2)}) async-start(), calls=%async_computation.3 | async-start | bytes 3145728 | tf_op jit(solution)/shard_map/while/body/eval_jaxpr/psum | solution.py:152
  963.7 114.6 %all-reduce.25.cloned.1.call-start = ((), (), s32[]{:S(2)}) async-start(), calls=%async_computation.4 | async-start | bytes 3145728 | tf_op jit(solution)/shard_map/while/body/eval_jaxpr/psum | solution.py:160
  1091.2 15.9 all-to-all-start
  1109.0 11.6 all-to-all-start.1
  1124.7 2168.8 %copy-start.43 = (f32[6,768]{1,0:T(8,128)S(1)}, f32[6,768]{1,0:T(8,128)}, u32[]{:S(2)}) copy-start(f32[6,768]{1,0:T(8,128)} %param.24) | copy-start | bytes 55300
  1124.7 2168.8 %copy-start.44 = (f32[6,768]{1,0:T(8,128)S(1)}, f32[6,768]{1,0:T(8,128)}, u32[]{:S(2)}) copy-start(f32[6,768]{1,0:T(8,128)} %param.25) | copy-start | bytes 55300
  1124.9 248.6 %all-reduce.27.cloned.1.call-start = ((), (), s32[]{:S(2)}) async-start(), calls=%async_computation.5 | async-start | bytes 14168064 | tf_op jit(solution)/shard_map/while
  1146.2 454.4 %all-reduce.29.cloned.1.call-start = ((), (), s32[]{:S(2)}) async-start(), calls=%async_computation.6 | async-start | bytes 3145728 | tf_op jit(solution)/shard_map/while/body/eval_jaxpr/psum | solution.py:245
  1531.5 215.7 %all-reduce.33.cloned.1.call-start = ((), (), s32[]{:S(2)}) async-start(), calls=%async_computation.8 | async-start | bytes 3145728 | tf_op jit(solution)/shard_map/while/body/eval_jaxpr/psum | solution.py:285
  1663.0 479.2 %all-reduce.31.cloned.1.call-start = ((), (), s32[]{:S(2)}) async-start(), calls=%async_computation.7 | async-start | bytes 28329984 | tf_op jit(solution)/shard_map/while
  1747.2 398.8 %copy-start.35 = (f32[6,768]{1,0:T(8,128)S(1)}, f32[6,768]{1,0:T(8,128)}, u32[]{:S(2)}) copy-start(f32[6,768]{1,0:T(8,128)} %copy-done.34) | copy-start | bytes 55300 | tf_op jit(solution)/shard_map/while
  2146.3 250.0 %all-reduce.27.cloned.1.call-start = ((), (), s32[]{:S(2)}) async-start(), calls=%async_computation.5 | async-start | bytes 14168064 | tf_op jit(solution)/shard_map/while
  2167.7 455.8 %all-reduce.29.cloned.1.call-start = ((), (), s32[]{:S(2)}) async-start(), calls=%async_computation.6 | async-start | bytes 3145728 | tf_op jit(solution)/shard_map/while/body/eval_jaxpr/psum | solution.py:245
  2554.1 215.9 %all-reduce.33.cloned.1.call-start = ((), (), s32[]{:S(2)}) async-start(), calls=%async_computation.8 | async-start | bytes 3145728 | tf_op jit(solution)/shard_map/while/body/eval_jaxpr/psum | solution.py:285
  2685.8 479.3 %all-reduce.31.cloned.1.call-start = ((), (), s32[]{:S(2)}) async-start(), calls=%async_computation.7 | async-start | bytes 28329984 | tf_op jit(solution)/shard_map/while
  2770.1 399.0 %copy-start.35 = (f32[6,768]{1,0:T(8,128)S(1)}, f32[6,768]{1,0:T(8,128)}, u32[]{:S(2)}) copy-start(f32[6,768]{1,0:T(8,128)} %copy-done.34) | copy-start | bytes 55300 | tf_op jit(solution)/shard_map/while
  2770.1 398.9 %copy-start.40 = (f32[2,2,6,512,1]{3,2,1,4,0:T(8,128)S(1)}, f32[2,2,6,512,1]{3,2,1,4,0:T(8,128)}, u32[]{:S(2)}) copy-start(f32[2,2,6,512,1]{3,2,1,4,0:T(8,128)} %copy-done.39) | copy-start | bytes 147460 | tf_op jit(solution)/shard_map/while
  (98 other events, 1003.7 us)
Sparse Core Ops, SparseCore 0:
  40.0 231.9 all-reduce.20
  429.8 19.4 all-reduce.22
  524.8 19.4 all-reduce.24
  575.7 230.4 all-reduce.20
  963.9 19.4 all-reduce.22
  1058.8 19.4 all-reduce.24
  1146.4 227.0 all-reduce.26
  1531.7 19.4 all-reduce.28
  1663.2 19.4 all-reduce.32
  1745.9 396.3 all-reduce.30
  2167.8 228.4 all-reduce.26
  2554.3 19.4 all-reduce.28
  2686.0 19.4 all-reduce.32
  2768.7 396.4 all-reduce.30
where the time goes:
time: 3320 us; the launch traced here: 3310 us
  waiting for transfers between devices  1640 us (49%)
  local copies, waits for them, and re-layouts  1090 us (33%)
  matrix products  253 us (8%)
  other arithmetic  169 us (5%)
  blocking collectives  115 us (3%)
    while x20, waiting for transfers between devices  1600 us
    slice x12, local copies, waits for them, and re-layouts, unpack(): packed[offset:offset + height * extent].reshape(height, extent)  403 us
    while x242, local copies, waits for them, and re-layouts  374 us
    broadcast_in_dim x2, local copies, waits for them, and re-layouts, backward_step(): jnp.concatenate([w_qkv_grad.reshape(-1), w_attn_grad.reshape(-1), w_in_gr...  108 us
    psum x1, blocking collectives, per_device(): shared_total = lax.psum(shared_acc, 'dp')  75.8 us
    reshape x16, local copies, waits for them, and re-layouts, unpack(): packed[offset:offset + height * extent].reshape(height, extent)  70.3 us
  transfers between devices with their start and end apart: 16, of which 10 were waited for; matrix products, arithmetic and copies ran while one was open for 17% of the time, Pallas kernels for 0%

commit v1 on v0

v1 whole, which is shorter than its diff:
```python
from functools import partial
import math

import jax
import jax.numpy as jnp
from jax import lax
from jax.experimental import pallas as pl
from jax.experimental.pallas import tpu as pltpu
from jax.sharding import PartitionSpec as P

HEAD_DIM = 64
FF = 3072
ROW = 512
SEG = 32
RPM = 2
MB = 2
MP = 2
LANES = 128
ROWS_DEV = MB * RPM
ROWS_CORE = ROWS_DEV // MP


LOSS_SCALE = 1024.0
CLIP_NORM = 0.5
LEARN_RATE = 0.1
SHARED_RATE = 0.5
BETA_ONE = 0.9
BETA_TWO = 0.999
ADAM_EPS = 1e-08
DECAY = 0.01
NORM_EPS = 1e-12
STEP_COUNT = 10.0
TOP_PRECISION = lax.Precision.HIGHEST
MESH = pl.DeviceIdType.MESH
DMA = pltpu.SemaphoreType.DMA
VMEM_LIMIT = 60 << 20


def normalize(values_in, scale_vec, shift_vec):
    center = jnp.mean(values_in, -1, keepdims=True)
    centered = values_in - center
    spread = jnp.mean(centered * centered, -1, keepdims=True)
    return centered * lax.rsqrt(spread + NORM_EPS) * scale_vec + shift_vec


def pair_loss(pair_items, labels):
    first_vec = pair_items[..., 0::2, :]
    second_vec = pair_items[..., 1::2, :]
    inner_prod = jnp.sum(first_vec * second_vec, -1)
    cosine = (
        inner_prod
        * lax.rsqrt(jnp.sum(first_vec * first_vec, -1) + 1e-06)
        * lax.rsqrt(jnp.sum(second_vec * second_vec, -1) + 1e-06)
    )
    error_term = cosine - labels.astype(jnp.float32) / 5.0
    return LOSS_SCALE * jnp.sum(error_term * error_term)


def adamw(weight, moment_one, moment_two, gradient, factor, step_count, rate):
    clipped = gradient * factor
    first_new = BETA_ONE * moment_one + (1.0 - BETA_ONE) * clipped
    second_new = BETA_TWO * moment_two + (1.0 - BETA_TWO) * clipped * clipped
    first_hat = first_new / (1.0 - BETA_ONE**step_count)
    second_hat = second_new / (1.0 - BETA_TWO**step_count)
    weight_new = weight - rate * (first_hat / (jnp.sqrt(second_hat) + ADAM_EPS) + DECAY * weight)
    return (weight_new, first_new, second_new)


class Layout:
    def __init__(self, features, shard, dp_count):
        self.features = features
        self.shard = shard
        self.dp_count = dp_count
        self.head_cols = features // MP
        self.ffn_cols = FF // MP
        self.total = shard * dp_count
        self.lines = self.total // LANES
        assert self.lines * LANES == self.total
        self.starts = [index * shard // LANES for index in range(dp_count)]
        need = max(
            ((index + 1) * shard - 1) // LANES - index * shard // LANES + 1
            for index in range(dp_count)
        )
        self.length = -(-need // 16) * 16
        self.cut = -(-self.length // 32) * 16
        self.mats = []
        offset = 0
        for height, extent in (
            (features, 3 * self.head_cols),
            (self.head_cols, features),
            (features, self.ffn_cols),
            (self.ffn_cols, features),
        ):
            assert extent % LANES == 0 and height % LANES == 0
            self.mats.append((offset, height, extent // LANES))
            offset += height * (extent // LANES)
        self.bias_start = offset
        self.bias_lines = self.lines - offset
        self.bias_rows = -(-self.bias_lines // 8) * 8
        self.flat_rows = -(-(self.starts[-1] + self.length) // 8) * 8


def weight_specs(lay):
    specs = [
        pl.BlockSpec((lay.features, 3 * lay.head_cols), lambda half: (0, half)),
        pl.BlockSpec((lay.head_cols, lay.features), lambda half: (half, 0)),
        pl.BlockSpec((lay.features, lay.ffn_cols), lambda half: (0, half)),
        pl.BlockSpec((lay.ffn_cols, lay.features), lambda half: (half, 0)),
        pl.BlockSpec((1, lay.bias_rows, LANES), lambda half: (half, 0, 0)),
    ]
    shapes = [
        (lay.features, MP * 3 * lay.head_cols),
        (MP * lay.head_cols, lay.features),
        (lay.features, MP * lay.ffn_cols),
        (MP * lay.ffn_cols, lay.features),
    ]
    return specs, shapes


def unpack_kernel(lay, lines_ref, qkv_ref, attn_ref, in_ref, out_ref, bias_ref, flat):
    for index in range(lay.dp_count):
        start = lay.starts[index]
        if index > 0:
            kept = flat[start : start + 1, :]
        flat[start : start + lay.length, :] = lines_ref[0, index].astype(jnp.float32)
        if index > 0:
            flat[start : start + 1, :] += kept
    for (offset, height, cols), ref in zip(lay.mats, (qkv_ref, attn_ref, in_ref, out_ref)):

        def body(step, carry, offset=offset, cols=cols, ref=ref):
            row = pl.multiple_of(step * LANES, LANES)
            for col in range(cols):
                block = flat[pl.ds(offset + row * cols + col, LANES, stride=cols), :]
                ref[pl.ds(row, LANES), col * LANES : (col + 1) * LANES] = block.astype(
                    jnp.bfloat16
                )
            return carry

        lax.fori_loop(0, height // LANES, body, 0)
    bias_ref[0] = flat[lay.bias_start : lay.bias_start + lay.bias_rows, :]


def unpack_weights(lay, gathered):
    specs, shapes = weight_specs(lay)
    return pl.pallas_call(
        partial(unpack_kernel, lay),
        grid=(MP,),
        in_specs=[
            pl.BlockSpec((1, lay.dp_count, lay.length, LANES), lambda half: (half, 0, 0, 0))
        ],
        out_specs=specs,
        out_shape=[jax.ShapeDtypeStruct(s, jnp.bfloat16) for s in shapes]
        + [jax.ShapeDtypeStruct((MP, lay.bias_rows, LANES), jnp.float32)],
        scratch_shapes=[pltpu.VMEM((lay.flat_rows, LANES), jnp.float32)],
        compiler_params=pltpu.CompilerParams(vmem_limit_bytes=VMEM_LIMIT),
        name="unpack_weights",
    )(gathered)


def pack_kernel(lay, qkv_ref, attn_ref, in_ref, out_ref, bias_ref, lines_ref, flat):
    for (offset, height, cols), ref in zip(lay.mats, (qkv_ref, attn_ref, in_ref, out_ref)):

        def body(step, carry, offset=offset, cols=cols, ref=ref):
            row = pl.multiple_of(step * LANES, LANES)
            for col in range(cols):
                block = ref[pl.ds(row, LANES), col * LANES : (col + 1) * LANES]
                flat[pl.ds(offset + row * cols + col, LANES, stride=cols), :] = block.astype(
                    jnp.float32
                )
            return carry

        lax.fori_loop(0, height // LANES, body, 0)
    tail = lay.flat_rows - lay.lines
    if tail:
        flat[lay.lines :, :] = jnp.zeros((tail, LANES), jnp.float32)
    flat[lay.bias_start : lay.lines, :] = bias_ref[0, : lay.bias_lines]
    for index in range(lay.dp_count):
        start = lay.starts[index]
        lines_ref[0, index] = flat[start : start + lay.length, :].astype(jnp.bfloat16)


def pack_gradients(lay, grads, bias_grad):
    specs, _ = weight_specs(lay)
    return pl.pallas_call(
        partial(pack_kernel, lay),
        grid=(MP,),
        in_specs=specs,
        out_specs=pl.BlockSpec(
            (1, lay.dp_count, lay.length, LANES), lambda half: (half, 0, 0, 0)
        ),
        out_shape=jax.ShapeDtypeStruct((MP, lay.dp_count, lay.length, LANES), jnp.bfloat16),
        scratch_shapes=[pltpu.VMEM((lay.flat_rows, LANES), jnp.float32)],
        compiler_params=pltpu.CompilerParams(vmem_limit_bytes=VMEM_LIMIT),
        name="pack_gradients",
    )(*grads, bias_grad)


class Place:
    def __init__(self):
        self.dp = lax.axis_index("dp")
        self.half = lax.axis_index("mp")
        self.z = self.dp // 4
        self.y = (self.dp // 2) % 2
        self.x = self.dp % 2
        self.has_up = self.z < 3
        self.has_down = self.z > 0
        self.up = (jnp.minimum(self.dp + 4, 12 + self.dp % 4), self.half)
        self.down = (jnp.maximum(self.dp - 4, self.dp % 4), self.half)
        self.xn = (self.shard(self.z, self.y, 1 - self.x), self.half)
        self.yn = (self.shard(self.z, 1 - self.y, self.x), self.half)
        self.sib = (self.dp, 1 - self.half)

    def shard(self, z, y, x):
        return z * 4 + y * 2 + x

    def barrier(self):
        bar = pltpu.get_barrier_semaphore()
        for dev in (self.xn, self.yn, self.sib):
            pl.semaphore_signal(bar, inc=1, device_id=dev, device_id_type=MESH)

        @pl.when(self.has_up)
        def _():
            pl.semaphore_signal(bar, inc=1, device_id=self.up, device_id_type=MESH)

        @pl.when(self.has_down)
        def _():
            pl.semaphore_signal(bar, inc=1, device_id=self.down, device_id_type=MESH)

        pl.semaphore_wait(
            bar, 3 + jnp.where(self.has_up, 1, 0) + jnp.where(self.has_down, 1, 0)
        )


def guarded(cond, work):
    if cond is None:
        work()
    else:
        pl.when(cond)(work)


def gather_kernel(
    lay, own_ref, buf, zs_sem, zr_sem, xs_sem, xr_sem, ys_sem, yr_sem, ss_sem, sr_sem, loc_sem
):
    at = Place()
    halves = ((0, lay.cut), (lay.cut, lay.length - lay.cut))
    local = pltpu.make_async_copy(own_ref, buf.at[at.half, at.dp], loc_sem)
    local.start()
    at.barrier()
    local.wait()
    sends = []

    def remote(index, part, send_sem, recv_sem, dev):
        piece = buf.at[at.half, index, pl.ds(*halves[part])]
        return pltpu.make_async_remote_copy(
            src_ref=piece,
            dst_ref=piece,
            send_sem=send_sem,
            recv_sem=recv_sem,
            device_id=dev,
            device_id_type=MESH,
        )

    def send(index, part, send_sem, recv_sem, dev, cond=None):
        guarded(cond, lambda: remote(index, part, send_sem, recv_sem, dev).start())
        sends.append((cond, lambda: remote(index, part, send_sem, recv_sem, dev).wait_send()))

    def wait(index, part, send_sem, recv_sem, dev, cond=None):
        guarded(cond, lambda: remote(index, part, send_sem, recv_sem, dev).wait_recv())

    def share(index, part, cond=None):
        send(index, part, ss_sem.at[index, part], sr_sem.at[index, part], at.sib, cond)

    for part in range(2):
        send(at.dp, part, zs_sem.at[0, 0, part], zr_sem.at[0, 1, part], at.up, at.has_up)
        send(at.dp, part, zs_sem.at[1, 0, part], zr_sem.at[1, 1, part], at.down, at.has_down)
        send(at.dp, part, xs_sem.at[at.z, part], xr_sem.at[at.z, part], at.xn)
        send(at.dp, part, ys_sem.at[at.z, part], yr_sem.at[at.z, part], at.yn)
        share(at.dp, part)

    def chain(dist):
        for part in range(2):
            for down in range(2):
                src = at.z + dist if down else at.z - dist
                ok = (src <= 3) if down else (src >= 0)
                src = jnp.clip(src, 0, 3)
                index = at.shard(src, at.y, at.x)
                dev = at.down if down else at.up
                onward = at.has_down if down else at.has_up
                wait(
                    index, part, zs_sem.at[down, 0, part], zr_sem.at[down, dist, part], dev, ok
                )
                if dist < 3:
                    send(
                        index,
                        part,
                        zs_sem.at[down, dist, part],
                        zr_sem.at[down, dist + 1, part],
                        dev,
                        ok & onward,
                    )
                send(index, part, xs_sem.at[src, part], xr_sem.at[src, part], at.xn, ok)
                send(index, part, ys_sem.at[src, part], yr_sem.at[src, part], at.yn, ok)
                share(index, part, ok)

    def sources(dist):
        if dist == 0:
            return [(at.z, None)]
        return [
            (jnp.clip(at.z - dist, 0, 3), at.z - dist >= 0),
            (jnp.clip(at.z + dist, 0, 3), at.z + dist <= 3),
        ]

    def plane(dist):
        for src, ok in sources(dist):
            for part in range(2):
                from_x = at.shard(src, at.y, 1 - at.x)
                from_y = at.shard(src, 1 - at.y, at.x)
                wait(from_x, part, xs_sem.at[src, part], xr_sem.at[src, part], at.xn, ok)
                if part == 0:
                    send(from_x, 0, ys_sem.at[src, 2], yr_sem.at[src, 2], at.yn, ok)
                share(from_x, part, ok)
                wait(from_y, part, ys_sem.at[src, part], yr_sem.at[src, part], at.yn, ok)
                if part == 1:
                    send(from_y, 1, xs_sem.at[src, 2], xr_sem.at[src, 2], at.xn, ok)
                share(from_y, part, ok)

    def diagonal(dist):
        for src, ok in sources(dist):
            index = at.shard(src, 1 - at.y, 1 - at.x)
            wait(index, 0, ys_sem.at[src, 2], yr_sem.at[src, 2], at.yn, ok)
            wait(index, 1, xs_sem.at[src, 2], xr_sem.at[src, 2], at.xn, ok)
            for part in range(2):
                share(index, part, ok)

    chain(1)
    plane(0)
    chain(2)
    plane(1)
    diagonal(0)
    chain(3)
    plane(2)
    diagonal(1)
    plane(3)
    diagonal(2)
    diagonal(3)
    for index in range(16):
        for part in range(2):
            piece = buf.at[1 - at.half, index, pl.ds(*halves[part])]
            pltpu.make_async_remote_copy(
                src_ref=piece,
                dst_ref=piece,
                send_sem=ss_sem.at[index, part],
                recv_sem=sr_sem.at[index, part],
                device_id=at.sib,
                device_id_type=MESH,
            ).wait_recv()
    for cond, work in sends:
        guarded(cond, work)


def gather_lines(lay, own):
    if lay.dp_count != 16:
        gathered = lax.all_gather(own, ("mp", "dp"), axis=0, tiled=True)
        return gathered.reshape(MP, lay.dp_count, lay.length, LANES)
    return pl.pallas_call(
        partial(gather_kernel, lay),
        out_shape=jax.ShapeDtypeStruct((MP, 16, lay.length, LANES), jnp.bfloat16),
        in_specs=[pl.BlockSpec(memory_space=pl.ANY)],
        out_specs=pl.BlockSpec(memory_space=pltpu.VMEM),
        scratch_shapes=[
            DMA((2, 4, 2)),
            DMA((2, 4, 2)),
            DMA((4, 3)),
            DMA((4, 3)),
            DMA((4, 3)),
            DMA((4, 3)),
            DMA((16, 2)),
            DMA((16, 2)),
            DMA,
        ],
        compiler_params=pltpu.CompilerParams(
            collective_id=0, has_side_effects=True, vmem_limit_bytes=VMEM_LIMIT
        ),
        name="gather_lines",
    )(own)


def scatter_kernel(
    lay,
    part_ref,
    out_ref,
    part,
    from_sib,
    from_x,
    from_y,
    diag_x,
    diag_y,
    from_z,
    acc_z,
    load_sem,
    ss_sem,
    sr_sem,
    xs_sem,
    xr_sem,
    ys_sem,
    yr_sem,
    zs_sem,
    zr_sem,
):
    at = Place()
    halves = ((0, lay.cut), (lay.cut, lay.length - lay.cut))
    my_part = part.at[at.half]

    def load(index):
        return [
            pltpu.make_async_copy(
                part_ref.at[half, index], part.at[half, index], load_sem.at[half, index]
            )
            for half in (0, 1)
        ]

    columns = (
        (1 - at.y, 1 - at.x),
        (at.y, 1 - at.x),
        (1 - at.y, at.x),
        (at.y, at.x),
    )
    order_z = (3, 0, 2, 1)
    order = [(z, col) for col in columns for z in order_z]
    for z, (y, x) in order:
        for copy in load(at.shard(z, y, x)):
            copy.start()
    at.barrier()
    sends = []

    def remote(src, dst, send_sem, recv_sem, dev):
        return pltpu.make_async_remote_copy(
            src_ref=src,
            dst_ref=dst,
            send_sem=send_sem,
            recv_sem=recv_sem,
            device_id=dev,
            device_id_type=MESH,
        )

    def send(copy, cond=None):
        guarded(cond, lambda: copy().start())
        sends.append((cond, lambda: copy().wait_send()))

    for z, (y, x) in order:
        index = at.shard(z, y, x)
        for copy in load(index):
            copy.wait()
        send(
            lambda index=index: remote(
                part.at[1 - at.half, index],
                from_sib.at[index],
                ss_sem.at[index],
                sr_sem.at[index],
                at.sib,
            )
        )

    def wait_sib(index):
        remote(
            my_part.at[index], from_sib.at[index], ss_sem.at[index], sr_sem.at[index], at.sib
        ).wait_recv()

    def wide(ref, span):
        return ref[pl.ds(*span), :].astype(jnp.float32)

    step_rows = 16 * math.gcd(lay.cut // 16, (lay.length - lay.cut) // 16)

    def add_into(dst, terms, span):
        def body(step, carry):
            rows = (pl.multiple_of(span[0] + step * step_rows, 16), step_rows)
            total = wide(terms[0], rows)
            for term in terms[1:]:
                total = total + wide(term, rows)
            dst[pl.ds(*rows), :] = total.astype(dst.dtype)
            return carry

        lax.fori_loop(0, span[1] // step_rows, body, 0)

    whole = (0, lay.length)
    for z in order_z:
        index = at.shard(z, 1 - at.y, 1 - at.x)
        wait_sib(index)
        mine = my_part.at[index]
        add_into(mine, [mine, from_sib.at[index]], whole)
        send(
            lambda z=z, mine=mine: remote(
                mine.at[pl.ds(*halves[0])], diag_y.at[z], ys_sem.at[z, 1], yr_sem.at[z, 1], at.yn
            )
        )
        send(
            lambda z=z, mine=mine: remote(
                mine.at[pl.ds(*halves[1])], diag_x.at[z], xs_sem.at[z, 1], xr_sem.at[z, 1], at.xn
            )
        )
    for z in order_z:
        index = at.shard(z, at.y, 1 - at.x)
        wait_sib(index)
        mine = my_part.at[index]
        remote(
            mine.at[pl.ds(*halves[0])], diag_y.at[z], ys_sem.at[z, 1], yr_sem.at[z, 1], at.yn
        ).wait_recv()
        add_into(mine, [mine, from_sib.at[index], diag_y.at[z]], halves[0])
        add_into(mine, [mine, from_sib.at[index]], halves[1])
        send(
            lambda z=z, mine=mine: remote(
                mine, from_x.at[z], xs_sem.at[z, 0], xr_sem.at[z, 0], at.xn
            )
        )
        index = at.shard(z, 1 - at.y, at.x)
        wait_sib(index)
        mine = my_part.at[index]
        remote(
            mine.at[pl.ds(*halves[1])], diag_x.at[z], xs_sem.at[z, 1], xr_sem.at[z, 1], at.xn
        ).wait_recv()
        add_into(mine, [mine, from_sib.at[index]], halves[0])
        shifted = diag_x.at[z]

        def body(step, carry, mine=mine, index=index, shifted=shifted):
            rows = pl.ds(pl.multiple_of(halves[1][0] + step * step_rows, 16), step_rows)
            base = pl.ds(pl.multiple_of(step * step_rows, 16), step_rows)
            total = (
                mine[rows, :].astype(jnp.float32)
                + from_sib[index, rows, :].astype(jnp.float32)
                + shifted[base, :].astype(jnp.float32)
            )
            mine[rows, :] = total.astype(jnp.bfloat16)
            return carry

        lax.fori_loop(0, halves[1][1] // step_rows, body, 0)
        send(
            lambda z=z, mine=mine: remote(
                mine, from_y.at[z], ys_sem.at[z, 0], yr_sem.at[z, 0], at.yn
            )
        )

    for z in order_z:
        index = at.shard(z, at.y, at.x)
        wait_sib(index)
        mine = my_part.at[index]
        remote(mine, from_x.at[z], xs_sem.at[z, 0], xr_sem.at[z, 0], at.xn).wait_recv()
        remote(mine, from_y.at[z], ys_sem.at[z, 0], yr_sem.at[z, 0], at.yn).wait_recv()
        base = [mine, from_sib.at[index], from_x.at[z], from_y.at[z]]

        for down in range(2):
            dev = at.down if down else at.up
            passes = (at.z > z) if down else (at.z < z)
            gets = (at.z < 3) if down else (at.z > 0)

            def arrive(z=z, mine=mine, down=down, dev=dev):
                remote(
                    mine, from_z.at[down, z], zs_sem.at[down, z], zr_sem.at[down, z], dev
                ).wait_recv()

            @pl.when(passes & gets)
            def _():
                arrive()
                add_into(acc_z.at[down, z], base + [from_z.at[down, z]], whole)

            @pl.when(passes & jnp.logical_not(gets))
            def _():
                add_into(acc_z.at[down, z], base, whole)

            send(
                lambda z=z, down=down, dev=dev: remote(
                    acc_z.at[down, z],
                    from_z.at[down, z],
                    zs_sem.at[down, z],
                    zr_sem.at[down, z],
                    dev,
                ),
                passes,
            )

    index = at.dp
    mine = my_part.at[index]
    base = [mine, from_sib.at[index], from_x.at[at.z], from_y.at[at.z]]
    add_into(out_ref, base, whole)
    for down in range(2):

        @pl.when((at.z < 3) if down else (at.z > 0))
        def _(down=down):
            arrived = from_z.at[down, at.z]
            dev = at.down if down else at.up
            remote(
                mine, arrived, zs_sem.at[down, at.z], zr_sem.at[down, at.z], dev
            ).wait_recv()
            add_into(out_ref, [out_ref, arrived], whole)

    for cond, work in sends:
        guarded(cond, work)


def scatter_lines(lay, packed):
    if lay.dp_count != 16:
        flat = packed.reshape(MP * lay.dp_count * lay.length, LANES)
        return lax.psum_scatter(
            flat, ("mp", "dp"), scatter_dimension=0, tiled=True
        ).astype(jnp.float32)
    size = (lay.length, LANES)
    low = jnp.bfloat16
    return pl.pallas_call(
        partial(scatter_kernel, lay),
        out_shape=jax.ShapeDtypeStruct(size, jnp.float32),
        in_specs=[pl.BlockSpec(memory_space=pl.ANY)],
        out_specs=pl.BlockSpec(memory_space=pltpu.VMEM),
        scratch_shapes=[
            pltpu.VMEM((MP, 16) + size, low),
            pltpu.VMEM((16,) + size, low),
            pltpu.VMEM((4,) + size, low),
            pltpu.VMEM((4,) + size, low),
            pltpu.VMEM((4, lay.length - lay.cut, LANES), low),
            pltpu.VMEM((4, lay.cut, LANES), low),
            pltpu.VMEM((2, 4) + size, low),
            pltpu.VMEM((2, 4) + size, low),
            DMA((MP, 16)),
            DMA((16,)),
            DMA((16,)),
            DMA((4, 2)),
            DMA((4, 2)),
            DMA((4, 2)),
            DMA((4, 2)),
            DMA((2, 4)),
            DMA((2, 4)),
        ],
        compiler_params=pltpu.CompilerParams(
            collective_id=1, has_side_effects=True, vmem_limit_bytes=VMEM_LIMIT
        ),
        name="scatter_lines",
    )(packed)


SCORE_SCALE = HEAD_DIM ** (-0.5)
LAST = (((1,), (1,)), ((), ()))
FIRST = (((0,), (0,)), ((), ()))


def attend_kernel(heads, qkv_ref, seg_col_ref, seg_row_ref, out_ref, log_ref):
    width = heads * HEAD_DIM
    same = seg_col_ref[...] == seg_row_ref[0]
    logs = []
    for head in range(heads):
        low = head * HEAD_DIM
        queries = qkv_ref[:, low : low + HEAD_DIM]
        keys = qkv_ref[:, width + low : width + low + HEAD_DIM]
        values = qkv_ref[:, 2 * width + low : 2 * width + low + HEAD_DIM]
        scores = lax.dot_general(queries, keys, LAST, preferred_element_type=jnp.float32)
        scores = jnp.where(same, scores * SCORE_SCALE, -1e30)
        row_max = jnp.max(scores, -1, keepdims=True)
        exponent = jnp.exp(scores - row_max)
        row_total = jnp.sum(exponent, -1, keepdims=True)
        probs = (exponent * (1.0 / row_total)).astype(jnp.bfloat16)
        mixed = jnp.dot(probs, values, preferred_element_type=jnp.float32)
        out_ref[:, low : low + HEAD_DIM] = mixed.astype(jnp.bfloat16)
        logs.append(row_max + jnp.log(row_total))
    log_ref[0] = jnp.concatenate(logs + [logs[0]] * (8 - heads), 1)


def attend(qkv, seg_col, seg_row, head_cols):
    heads = head_cols // HEAD_DIM
    rows = qkv.shape[0] // ROW
    return pl.pallas_call(
        partial(attend_kernel, heads),
        grid=(rows, MP),
        in_specs=[
            pl.BlockSpec((ROW, 3 * head_cols), lambda r, m: (r, m)),
            pl.BlockSpec((ROW, 1), lambda r, m: (r, 0)),
            pl.BlockSpec((1, 1, ROW), lambda r, m: (r, 0, 0)),
        ],
        out_specs=[
            pl.BlockSpec((ROW, head_cols), lambda r, m: (r, m)),
            pl.BlockSpec((1, ROW, 8), lambda r, m: (m, r, 0)),
        ],
        out_shape=[
            jax.ShapeDtypeStruct((rows * ROW, MP * head_cols), jnp.bfloat16),
            jax.ShapeDtypeStruct((MP, rows * ROW, 8), jnp.float32),
        ],
        compiler_params=pltpu.CompilerParams(vmem_limit_bytes=VMEM_LIMIT),
        name="attend",
    )(qkv, seg_col, seg_row)


def attend_back_kernel(heads, qkv_ref, grad_ref, log_ref, seg_col_ref, seg_row_ref, out_ref):
    width = heads * HEAD_DIM
    same = seg_col_ref[...] == seg_row_ref[0]
    for head in range(heads):
        low = head * HEAD_DIM
        queries = qkv_ref[:, low : low + HEAD_DIM]
        keys = qkv_ref[:, width + low : width + low + HEAD_DIM]
        values = qkv_ref[:, 2 * width + low : 2 * width + low + HEAD_DIM]
        mixed_grad = grad_ref[:, low : low + HEAD_DIM]
        scores = lax.dot_general(queries, keys, LAST, preferred_element_type=jnp.float32)
        scores = jnp.where(same, scores * SCORE_SCALE, -1e30)
        probs = jnp.exp(scores - log_ref[0, :, head : head + 1])
        prob_grad = lax.dot_general(
            mixed_grad, values, LAST, preferred_element_type=jnp.float32
        )
        row_inner = jnp.sum(prob_grad * probs, -1, keepdims=True)
        score_grad = (probs * (prob_grad - row_inner)).astype(jnp.bfloat16)
        value_grad = lax.dot_general(
            probs.astype(jnp.bfloat16), mixed_grad, FIRST, preferred_element_type=jnp.float32
        )
        query_grad = (
            jnp.dot(score_grad, keys, preferred_element_type=jnp.float32) * SCORE_SCALE
        )
        key_grad = (
            lax.dot_general(score_grad, queries, FIRST, preferred_element_type=jnp.float32)
            * SCORE_SCALE
        )
        for place, value in enumerate((query_grad, key_grad, value_grad)):
            start = place * width + low
            out_ref[:, start : start + HEAD_DIM] = value.astype(jnp.bfloat16)


def attend_back(qkv, mixed_grad, logs, seg_col, seg_row, head_cols):
    heads = head_cols // HEAD_DIM
    rows = qkv.shape[0] // ROW
    return pl.pallas_call(
        partial(attend_back_kernel, heads),
        grid=(rows, MP),
        in_specs=[
            pl.BlockSpec((ROW, 3 * head_cols), lambda r, m: (r, m)),
            pl.BlockSpec((ROW, head_cols), lambda r, m: (r, m)),
            pl.BlockSpec((1, ROW, 8), lambda r, m: (m, r, 0)),
            pl.BlockSpec((ROW, 1), lambda r, m: (r, 0)),
            pl.BlockSpec((1, 1, ROW), lambda r, m: (r, 0, 0)),
        ],
        out_specs=pl.BlockSpec((ROW, 3 * head_cols), lambda r, m: (r, m)),
        out_shape=jax.ShapeDtypeStruct(qkv.shape, jnp.bfloat16),
        compiler_params=pltpu.CompilerParams(vmem_limit_bytes=VMEM_LIMIT),
        name="attend_back",
    )(qkv, mixed_grad, logs, seg_col, seg_row)


def back_norm(values_in, scale_vec, grad):
    center = jnp.mean(values_in, -1, keepdims=True)
    centered = values_in - center
    inverse = lax.rsqrt(jnp.mean(centered * centered, -1, keepdims=True) + NORM_EPS)
    unit = centered * inverse
    scaled = grad * scale_vec
    out = inverse * (
        scaled
        - jnp.mean(scaled, -1, keepdims=True)
        - unit * jnp.mean(scaled * unit, -1, keepdims=True)
    )
    return out, jnp.sum(grad * unit, 0), jnp.sum(grad, 0)


def per_device(
    tokens,
    segments,
    sentence_dest,
    pair_source,
    labels,
    params,
    first,
    second,
    shared,
    shared_first,
    shared_second,
):
    features = tokens.shape[1]
    dp_count = lax.axis_size("dp")
    dp_index = lax.axis_index("dp")
    mp_index = lax.axis_index("mp")
    shard = params.shape[1]
    lay = Layout(features, shard, dp_count)
    head_cols = lay.head_cols
    sent_slots = ROWS_DEV * SEG
    slot_capacity = max(2, sent_slots // dp_count)
    params_total = MP * shard * dp_count + 6 * features
    core_rows = ROWS_CORE * ROW

    phase = (dp_index * shard) % LANES
    own = lax.dynamic_update_slice(
        jnp.zeros((lay.length * LANES,), jnp.bfloat16),
        params.astype(jnp.bfloat16).reshape(-1),
        (phase,),
    ).reshape(lay.length, LANES)
    w_qkv, w_attn, w_in, w_out, biases = unpack_weights(lay, gather_lines(lay, own))
    head_lines = head_cols // LANES
    b_query = biases[:, :head_lines].reshape(MP, head_cols)
    b_value = biases[:, head_lines : 2 * head_lines].reshape(MP, head_cols)
    b_in = biases[:, 2 * head_lines : lay.bias_lines].reshape(MP * lay.ffn_cols)
    b_qkv = jnp.concatenate([b_query, jnp.zeros_like(b_query), b_value], 1).reshape(-1)

    tokens_core = lax.dynamic_slice_in_dim(tokens, mp_index * core_rows, core_rows, 0)
    segments_core = lax.dynamic_slice_in_dim(segments, mp_index * core_rows, core_rows, 0)
    seg_col = segments_core.reshape(core_rows, 1)
    seg_row = segments_core.reshape(ROWS_CORE, 1, ROW)

    qkv = (jnp.dot(tokens_core, w_qkv, preferred_element_type=jnp.float32) + b_qkv).astype(
        jnp.bfloat16
    )
    mixed, logs = attend(qkv, seg_col, seg_row, head_cols)
    attn_out = jnp.dot(mixed, w_attn, preferred_element_type=jnp.float32) + shared[4]
    resid_one = tokens_core.astype(jnp.float32) + attn_out
    hidden = normalize(resid_one, shared[0], shared[1])
    hidden_low = hidden.astype(jnp.bfloat16)
    up_proj = jnp.dot(hidden_low, w_in, preferred_element_type=jnp.float32) + b_in
    cdf = 0.5 * (1.0 + lax.erf(up_proj * (0.5**0.5)))
    activated = (up_proj * cdf).astype(jnp.bfloat16)
    slope = (
        cdf + up_proj * jnp.exp(-0.5 * up_proj * up_proj) * ((2.0 * math.pi) ** -0.5)
    ).astype(jnp.bfloat16)
    ffn_out = jnp.dot(activated, w_out, preferred_element_type=jnp.float32) + shared[5]
    resid_two = hidden + ffn_out
    encoded_core = normalize(resid_two, shared[2], shared[3])
    encoded = lax.all_gather(encoded_core.astype(jnp.bfloat16), "mp", axis=0, tiled=True)

    slot_ids = jnp.arange(SEG, dtype=jnp.int32)
    onehot = (seg_row == slot_ids[None, :, None]).astype(jnp.float32)
    weight = onehot / jnp.sum(onehot, 2, keepdims=True)
    pooled_core = jnp.einsum(
        "kvf,kfo->kvo",
        weight,
        encoded_core.reshape(ROWS_CORE, ROW, features),
        precision=TOP_PRECISION,
    ).astype(jnp.bfloat16)
    pooled_flat = lax.all_gather(
        pooled_core.reshape(ROWS_CORE * SEG, features), "mp", axis=0, tiled=True
    )
    code_ids = jnp.arange(dp_count * slot_capacity, dtype=jnp.int32)
    send_code = sentence_dest[:, 0] * slot_capacity + sentence_dest[:, 1]
    send_map = (code_ids[:, None] == send_code[None, :]).astype(jnp.bfloat16)
    outgoing = jnp.dot(send_map, pooled_flat, preferred_element_type=jnp.float32).astype(
        jnp.bfloat16
    )
    outgoing = outgoing.reshape(dp_count, slot_capacity, features)
    incoming = lax.all_to_all(outgoing, "dp", split_axis=0, concat_axis=0, tiled=True).reshape(
        dp_count * slot_capacity, features
    )
    take_code = pair_source[:, 0] * slot_capacity + pair_source[:, 1]
    take_map = (take_code[:, None] == code_ids[None, :]).astype(jnp.bfloat16)
    pair_items = jnp.dot(take_map, incoming, preferred_element_type=jnp.float32)
    item_grad = jax.grad(pair_loss)(pair_items, labels).astype(jnp.bfloat16)
    returning = jnp.dot(take_map.T, item_grad, preferred_element_type=jnp.float32).astype(
        jnp.bfloat16
    )
    returning = returning.reshape(dp_count, slot_capacity, features)
    arrived = lax.all_to_all(returning, "dp", split_axis=0, concat_axis=0, tiled=True).reshape(
        dp_count * slot_capacity, features
    )
    core_map = lax.dynamic_slice_in_dim(send_map, mp_index * ROWS_CORE * SEG, ROWS_CORE * SEG, 1)
    pooled_grad = jnp.dot(core_map.T, arrived, preferred_element_type=jnp.float32)

    encoded_grad = jnp.einsum(
        "jix,jip->jxp",
        weight,
        pooled_grad.reshape(ROWS_CORE, SEG, features),
        precision=TOP_PRECISION,
    ).reshape(core_rows, features)
    resid_two_grad, scale_two, shift_two = back_norm(resid_two, shared[2], encoded_grad)
    ffn_grad = resid_two_grad.astype(jnp.bfloat16)
    act_grad = lax.dot_general(ffn_grad, w_out, LAST, preferred_element_type=jnp.float32)
    up_grad = (act_grad * slope.astype(jnp.float32)).astype(jnp.bfloat16)
    w_out_grad = lax.dot_general(activated, ffn_grad, FIRST, preferred_element_type=jnp.float32)
    w_in_grad = lax.dot_general(hidden_low, up_grad, FIRST, preferred_element_type=jnp.float32)
    hidden_term = lax.dot_general(up_grad, w_in, LAST, preferred_element_type=jnp.float32)
    hidden_grad = resid_two_grad + hidden_term
    resid_one_grad, scale_one, shift_one = back_norm(resid_one, shared[0], hidden_grad)
    attn_grad = resid_one_grad.astype(jnp.bfloat16)
    w_attn_grad = lax.dot_general(mixed, attn_grad, FIRST, preferred_element_type=jnp.float32)
    mixed_grad = lax.dot_general(
        attn_grad, w_attn, LAST, preferred_element_type=jnp.float32
    ).astype(jnp.bfloat16)
    qkv_grad = attend_back(qkv, mixed_grad, logs, seg_col, seg_row, head_cols)
    w_qkv_grad = lax.dot_general(
        tokens_core, qkv_grad, FIRST, preferred_element_type=jnp.float32
    )
    input_term = lax.dot_general(qkv_grad, w_qkv, LAST, preferred_element_type=jnp.float32)
    input_core = resid_one_grad + input_term
    input_grad = lax.all_gather(input_core, "mp", axis=0, tiled=True)

    qkv_sums = jnp.sum(qkv_grad.astype(jnp.float32), 0).reshape(MP, 3, head_lines, LANES)
    in_sums = jnp.sum(up_grad.astype(jnp.float32), 0).reshape(MP, -1, LANES)
    bias_grad = jnp.concatenate([qkv_sums[:, 0], qkv_sums[:, 2], in_sums], 1)
    bias_grad = jnp.pad(bias_grad, ((0, 0), (0, lay.bias_rows - lay.bias_lines), (0, 0)))
    packed = pack_gradients(
        lay,
        [g.astype(jnp.bfloat16) for g in (w_qkv_grad, w_attn_grad, w_in_grad, w_out_grad)],
        bias_grad,
    )
    grad_lines = scatter_lines(lay, packed)
    flat_grad = lax.dynamic_slice(grad_lines.reshape(-1), (phase,), (shard,))[None]
    flat_grad = flat_grad / LOSS_SCALE
    shared_step = jnp.stack(
        [
            scale_one,
            shift_one,
            scale_two,
            shift_two,
            jnp.sum(attn_grad.astype(jnp.float32), 0),
            jnp.sum(ffn_grad.astype(jnp.float32), 0),
        ]
    )
    shared_grad = lax.psum(shared_step, ("dp", "mp")) / LOSS_SCALE
    local_squares = jnp.sum(flat_grad * flat_grad)
    total_squares = lax.psum(local_squares, ("dp", "mp"))
    norm_value = jnp.sqrt(total_squares + jnp.sum(shared_grad * shared_grad))
    factor = jnp.minimum(1.0, CLIP_NORM / norm_value)
    step_count = STEP_COUNT
    params_new, first_new, second_new = adamw(
        params, first, second, flat_grad, factor, step_count, LEARN_RATE
    )
    shared_new, shared_first_new, shared_second_new = adamw(
        shared, shared_first, shared_second, shared_grad, factor, step_count, SHARED_RATE
    )
    grad_unit = math.sqrt(params_total) / CLIP_NORM
    params_grad = flat_grad * factor * grad_unit
    shared_grad_out = shared_grad * factor * grad_unit
    return (
        encoded,
        input_grad,
        norm_value.reshape(1),
        params_new,
        first_new,
        second_new,
        params_new.astype(jnp.bfloat16),
        shared_new,
        shared_first_new,
        shared_second_new,
        params_grad,
        shared_grad_out,
    )


def solution(mesh):
    in_specs = (
        P("dp", None),
        P("dp"),
        P("dp", None),
        P("dp", None),
        P("dp"),
        P("mp", "dp"),
        P("mp", "dp"),
        P("mp", "dp"),
        P(),
        P(),
        P(),
    )
    out_specs = (
        P("dp", None),
        P("dp", None),
        P(),
        P("mp", "dp"),
        P("mp", "dp"),
        P("mp", "dp"),
        P("mp", "dp"),
        P(),
        P(),
        P(),
        P("mp", "dp"),
        P(),
    )
    return jax.shard_map(
        per_device, mesh=mesh, in_specs=in_specs, out_specs=out_specs, check_vma=False
    )
```

time: 3320 us -> 489 us (0.15)
  waiting for transfers between devices: 1640 us -> 17.9 us
  local copies, waits for them, and re-layouts: 1090 us -> 27.6 us
  Pallas kernels: 0 us -> 219 us
  matrix products: 253 us -> 106 us
  other arithmetic: 169 us -> 33.7 us
  blocking collectives: 115 us -> 53.3 us
    while x20 -> x0, waiting for transfers between devices: 1600 us -> none
    slice x20 -> x2, local copies, waits for them, and re-layouts: 408 us -> 0.79 us  [the longest x1 0.74 us: per_device(): b_in = biases[:, 2 * head_lines:lay.bias_lines].reshape(MP * lay.ffn_cols)]
    while x242 -> x0, local copies, waits for them, and re-layouts: 374 us -> none
    pallas_call x0 -> x6, Pallas kernels: none -> 219 us  [the longest x1 74.7 us: scatter_lines(): pl.pallas_call(partial(scatter_kernel, lay), out_shape=jax.ShapeDtypeStru...]
    dot_general x43 -> x15, matrix products: 251 us -> 102 us  [the longest x1 13.2 us: per_device(): lax.dot_general(ffn_grad, w_out, LAST, preferred_element_type=jnp.float32)]
    reshape x41 -> x4, local copies, waits for them, and re-layouts: 123 us -> 1.04 us  [the longest x1 1.03 us: per_device(): seg_col = segments_core.reshape(core_rows, 1)]
    broadcast_in_dim x8 -> x2, local copies, waits for them, and re-layouts: 117 us -> 0.03 us  [the longest x1 0.03 us: per_device(): jnp.zeros((lay.length * LANES,), jnp.bfloat16)]
    psum x1 -> x0, blocking collectives: 75.8 us -> none  [per_device(): shared_total = lax.psum(shared_acc, 'dp')]
  transfers between devices with their start and end apart: 16 -> 4, of which waited for: 10 -> 3; matrix products, arithmetic and copies ran while one was open for 17% -> 19% of each run, Pallas kernels for 0% -> 23%
where the time goes in v1:
time: 489 us; the launch traced here: 485 us
  Pallas kernels  219 us (45%)
  matrix products  106 us (22%)
  blocking collectives  53.3 us (11%)
  other arithmetic  33.7 us (7%)
  local copies, waits for them, and re-layouts  27.6 us (6%)
  waiting for transfers between devices  17.9 us (4%)
  between operations  17.8 us (4%)
  starting transfers between devices  9.46 us (2%)
    pallas_call x1, Pallas kernels, scatter_lines(): pl.pallas_call(partial(scatter_kernel, lay), out_shape=jax.ShapeDtypeStru...  74.7 us
    pallas_call x1, Pallas kernels, gather_lines(): pl.pallas_call(partial(gather_kernel, lay), out_shape=jax.ShapeDtypeStruc...  70.3 us
    psum x1, blocking collectives, per_device(): total_squares = lax.psum(local_squares, ('dp', 'mp'))  51.2 us
    pallas_call x1, Pallas kernels, attend_back(): pl.pallas_call(partial(attend_back_kernel, heads), grid=(rows, MP), in_sp...  28.9 us
    pallas_call x1, Pallas kernels, attend(): pl.pallas_call(partial(attend_kernel, heads), grid=(rows, MP), in_specs=[...  24.3 us
    dot_general x1, matrix products, per_device(): lax.dot_general(ffn_grad, w_out, LAST, preferred_element_type=jnp.float32)  13.2 us
    dot_general x1, matrix products, per_device(): jnp.dot(hidden_low, w_in, preferred_element_type=jnp.float32) + b_in  12.1 us
    unnamed x80, local copies, waits for them, and re-layouts  11 us
  transfers between devices with their start and end apart: 4, of which 3 were waited for; matrix products, arithmetic and copies ran while one was open for 19% of the time, Pallas kernels for 23%

profile of v1, /device:TPU:0, one launch (start us, length us, event | category | flops | bytes accessed | tf_op | source)
XLA Modules:
  0.0 484.8 jit_solution(17553469690420070486)
XLA Ops:
  7.2 7.5 %convert_reduce_fusion.4 = bf16[221328]{0:T(1024)(128)(2,1)S(1)} fusion(f32[1,221328]{1,0:T(1,128)} %param.16), kind=kLoop, calls=%fused_computation.52 | loop fusion | flops 221328 | bytes 1327968 | tf_op jit(solution)/shard_map/convert_element_type | solution.py:782
  14.7 4.1 dynamic_update_slice.3
  19.6 70.3 %gather_lines.1.lines_ref = bf16[2,16,1744,128]{3,2,1,0:T(8,128)(2,1)} custom-call(bf16[1744,128]{1,0:T(8,128)(2,1)} %bitcast.78), custom_call_target="tpu_custom_call" | custom-call | tf_op jit(solution)/shard_map/gather_lines/pallas_call | solution.py:365
  90.0 10.6 %unpack_weights.1 = (bf16[768,2304]{1,0:T(8,128)(2,1)}, bf16[768,768]{1,0:T(8,128)(2,1)}, bf16[768,3072]{1,0:T(8,128)(2,1)}, bf16[3072,768]{1,0:T(8,128)(2,1)}, f32[2,24,128]{2,1,0:T(8,128)}) custom-call(bf16[2,16,1744,128]{3,2,1,0:T(8,128)(2,1)} %gather_lines.1.lines_ref), custom_call_target="tpu_custom_call" | custom-call | tf_op jit(solution)/shard_map/unpack_weights/pallas_call | solution.py:145
  103.3 8.4 %add_convert_fusion.qkv_ref = bf16[1024,2304]{1,0:T(8,128)(2,1)} fusion(bf16[768,2304]{1,0:T(8,128)(2,1)} %get-tuple-element.19, f32[2304]{0:T(1024)S(1)} %add.181, bf16[2048,768]{1,0:T(8,128)(2,1)} %param.11, s32[]{:T(128)S(6)} %select_n.18), kind=kOutput, calls=%fused_computation.11 | convolution fusion | flops 3628597248 | bytes 9839620 | tf_op jit(solution)/shard_map/dot_general | solution.py:797
  111.7 24.3 %attend.1 = (bf16[1024,768]{1,0:T(8,128)(2,1)}, f32[2,1024,8]{2,1,0:T(8,128)}) custom-call(bf16[1024,2304]{1,0:T(8,128)(2,1)} %add_convert_fusion.qkv_ref, s32[1024,1]{1,0:T(8,128)} %copy.23.seg_col_ref, s32[2,1,512]{2,1,0:T(1,128)} %bitcast.81), custom_call_target="tpu_custom_call" | custom-call | tf_op jit(solution)/shard_map/attend/pallas_call | solution.py:667
  140.4 12.1 %multiply_convert_fusion.1 = (bf16[1024,3072]{1,0:T(8,128)(2,1)S(1)}, f32[1024,3072]{1,0:T(8,128)}) fusion(f32[3072]{0:T(1024)S(1)} %add.192, bf16[768,3072]{1,0:T(8,128)(2,1)} %get-tuple-element.23, f32[1024,768]{1,0:T(8,128)S(1)} %get-tuple-element.73, f32[768]{0:T(1024)S(1)} %get-tuple-element.39, f32[768]{0:T(1024)S(1)} %get-tuple-element.40, ...), kind=kOutput, calls=%fused_computation.8 | convolution fusion | flops 4854644736 | bytes 26765312 | tf_op jit(solution)/shard_map/dot_general | solution.py:805
  152.5 10.9 %fusion.39 = (f32[1024]{0:T(1024)S(1)}, f32[1024,768]{1,0:T(8,128)S(1)}) fusion(f32[768]{0:T(1024)S(1)} %get-tuple-element.38, bf16[1024,3072]{1,0:T(8,128)(2,1)S(1)} %get-tuple-element.74, bf16[3072,768]{1,0:T(8,128)(2,1)} %get-tuple-element.24, f32[768]{0:T(1024)S(1)} %get-tuple-element.39, f32[768]{0:T(1024)S(1)} %get-tuple-element.40, ...), kind=kOutput, calls=%fused_computation.130 | convolution fusion | flops 4837342208 | bytes 17323008 | tf_op jit(solution)/shard_map/dot_general | solution.py:811
  170.9 5.9 %all-to-all-start = ((bf16[16,8,768]{2,1,0:T(8,128)(2,1)}), bf16[16,8,768]{2,1,0:T(8,128)(2,1)S(1)}, u32[]{:S(2)}, u32[]{:S(2)}) async-start(bf16[16,8,768]{2,1,0:T(8,128)(2,1)} %fusion.9), calls=%async_computation | async-start | bytes 393216 | tf_op jit(solution)/shard_map/all_to_all | solution.py:835
  176.8 9.1 %all-to-all-done = bf16[16,8,768]{2,1,0:T(8,128)(2,1)S(1)} async-done(((bf16[16,8,768]{2,1,0:T(8,128)(2,1)}), bf16[16,8,768]{2,1,0:T(8,128)(2,1)S(1)}, u32[]{:S(2)}, u32[]{:S(2)}) %all-to-all-start) | async-done | bytes 196640 | tf_op jit(solution)/shard_map/all_to_all | solution.py:835
  201.3 6.5 %all-to-all-done.1 = bf16[16,8,768]{2,1,0:T(8,128)(2,1)S(1)} async-done(((bf16[16,8,768]{2,1,0:T(8,128)(2,1)}), bf16[16,8,768]{2,1,0:T(8,128)(2,1)S(1)}, u32[]{:S(2)}, u32[]{:S(2)}) %all-to-all-start.1) | async-done | bytes 196640 | tf_op jit(solution)/shard_map/all_to_all | solution.py:846
  214.4 7.1 %convolution_convert_fusion.out_ref = bf16[3072,768]{1,0:T(8,128)(2,1)} fusion(bf16[1024,3072]{1,0:T(8,128)(2,1)S(1)} %bitcast.90, f32[1024,768]{1,0:T(8,128)S(1)} %get-tuple-element.53), kind=kOutput, calls=%fused_computation.12 | convolution fusion | flops 4834983936 | bytes 14155776 | tf_op jit(solution)/shard_map/dot_general | solution.py:862
  221.6 13.2 %convert_reduce_fusion = (f32[3072]{0:T(1024)S(1)}, bf16[1024,3072]{1,0:T(8,128)(2,1)}) fusion(f32[1024,3072]{1,0:T(8,128)} %get-tuple-element.75, f32[3072]{0:T(1024)S(1)} %copy-done.20, bf16[3072,768]{1,0:T(8,128)(2,1)S(1)} %bitcast.88, f32[1024,768]{1,0:T(8,128)S(1)} %get-tuple-element.53), kind=kOutput, calls=%fused_computation.6 | convolution fusion | flops 4879807488 | bytes 26763264 | tf_op jit(solution)/shard_map/dot_general | solution.py:860
  234.9 8.3 %multiply_reduce_fusion = (f32[768]{0:T(1024)S(1)}, f32[1024]{0:T(1024)S(1)}, f32[1024]{0:T(1024)S(1)}, f32[768]{0:T(1024)S(1)}, f32[1024,768]{1,0:T(8,128)S(1)}) fusion(f32[1024,768]{1,0:T(8,128)S(1)} %copy-done.2, f32[1024]{0:T(1024)S(1)} %copy-done.16, f32[1024]{0:T(1024)S(1)} %copy-done.12, f32[768]{0:T(1024)S(1)} %copy-done.18, ...), kind=kOutput, calls=%fused_computation.20 | convolution fusion | flops 4839698432 | bytes 20472832 | tf_op jit(solution)/shard_map/dot_general | solution.py:864
  243.2 10.0 %convolution_convert_fusion.1.in_ref = bf16[768,3072]{1,0:T(8,128)(2,1)} fusion(bf16[1024,3072]{1,0:T(8,128)(2,1)} %get-tuple-element.81, f32[1024,768]{1,0:T(8,128)S(1)} %copy-done.2, f32[768]{0:T(1024)S(1)} %copy-done.23, f32[768]{0:T(1024)S(1)} %copy-done.18, f32[1024]{0:T(1024)S(1)} %copy-done.16, f32[1024]{0:T(1024)S(1)} %copy-done.12), kind=kOutput, calls=%fused_computation.13 | convolution fusion | flops 4838129664 | bytes 14170112 | tf_op jit(solution)/shard_map/dot_general | solution.py:863
  259.8 28.9 %attend_back.1 = bf16[1024,2304]{1,0:T(8,128)(2,1)} custom-call(bf16[1024,2304]{1,0:T(8,128)(2,1)} %add_convert_fusion.qkv_ref, bf16[1024,768]{1,0:T(8,128)(2,1)} %convolution_convert_fusion.3.grad_ref, f32[2,1024,8]{2,1,0:T(8,128)} %get-tuple-element.25.log_ref, s32[1024,1]{1,0:T(8,128)} %copy.23.seg_col_ref, s32[2,1,512]{2,1,0:T(1,128)} %bitcast.82), custom_call_target="tpu_custom_call" | custom-call | tf_op jit(solution)/shard_map/attend_back/pallas_call | solution.py:723
  292.4 7.4 %convolution_convert_fusion.2.qkv_ref = bf16[768,2304]{1,0:T(8,128)(2,1)} fusion(bf16[1024,2304]{1,0:T(8,128)(2,1)S(1)} %copy-done, bf16[2048,768]{1,0:T(8,128)(2,1)} %param.11, s32[]{:T(128)S(6)} %select_n.18), kind=kOutput, calls=%fused_computation.14 | convolution fusion | flops 3625648128 | bytes 9830404 | tf_op jit(solution)/shard_map/dot_general | solution.py:873
  300.5 10.1 %pack_gradients.1.part_ref = bf16[2,16,1744,128]{3,2,1,0:T(8,128)(2,1)} custom-call(bf16[768,2304]{1,0:T(8,128)(2,1)} %convolution_convert_fusion.2.qkv_ref, bf16[768,768]{1,0:T(8,128)(2,1)} %convolution_convert_fusion.4.attn_ref, bf16[768,3072]{1,0:T(8,128)(2,1)} %convolution_convert_fusion.1.in_ref, bf16[3072,768]{1,0:T(8,128)(2,1)} %convolution_convert_fusion.out_ref, ...), custom_call_target="tpu_custom_call" | custom-call | tf_op jit(solution)/shard_map/pack_gradients/pallas_call | solution.py:184
  310.6 74.7 %scatter_lines.1 = f32[1744,128]{1,0:T(8,128)} custom-call(bf16[2,16,1744,128]{3,2,1,0:T(8,128)(2,1)} %pack_gradients.1.part_ref), custom_call_target="tpu_custom_call" | custom-call | tf_op jit(solution)/shard_map/scatter_lines/pallas_call | solution.py:607
  387.5 9.9 %convolution_add_fusion.1 = f32[1024,768]{1,0:T(8,128)} fusion(f32[1024,768]{1,0:T(8,128)} %copy-done.6, bf16[1024,2304]{1,0:T(8,128)(2,1)} %attend_back.1, bf16[768,2304]{1,0:T(8,128)(2,1)} %get-tuple-element.19), kind=kOutput, calls=%fused_computation.37 | convolution fusion | flops 3624665088 | bytes 14548992 | tf_op jit(solution)/shard_map/dot_general | solution.py:876
  397.4 51.2 %all-reduce.3 = (f32[]{:T(128)}, f32[6,768]{1,0:T(8,128)S(1)}) all-reduce(f32[]{:T(128)} %multiply_reduce_fusion.7, f32[6,768]{1,0:T(8,128)S(1)} %stack.27), channel_id=1, replica_groups=mesh['dp'=16,'mp'=2] {'dp','mp'}, use_global_device_ids=true, to_apply=%region_15.16 | all-reduce | flops 4609 | bytes 36872 | tf_op jit(solution)/shard_map/psum | solution.py:904
  453.0 8.7 %fusion.36 = (bf16[1,221328]{1,0:T(2,128)(2,1)}, f32[1,221328]{1,0:T(1,128)}, f32[1,221328]{1,0:T(1,128)}, f32[1,221328]{1,0:T(1,128)}) fusion(f32[1,221328]{1,0:T(1,128)} %param.16, f32[221328]{0:T(1024)S(1)} %copy-done.5, f32[1,221328]{1,0:T(1,128)} %param.17, f32[221328]{0:T(1024)S(1)} %get-tuple-element.61, f32[1,221328]{1,0:T(1,128)} %param.18), kind=kLoop, calls=%fused_computation.127 | loop fusion | flops 2877264 | bytes 7525152 | tf_op jit(solution)/shard_map/convert_element_type | solution.py:924
  461.7 4.9 %mul.440 = f32[1,221328]{1,0:T(1,128)} reshape(f32[221328]{0:T(1024)S(1)} %get-tuple-element.60) | data formatting | bytes 1770624 | tf_op jit(solution)/shard_map/mul | solution.py:915
  468.8 3.9 copy.41
  (154 shorter events, 59.0 us)
Async XLA Ops:
  90.0 12.2 %copy-start.26 = (s32[2048]{0:T(1024)S(1)}, s32[2048]{0:T(1024)}, u32[]{:S(2)}) copy-start(s32[2048]{0:T(1024)} %param.12) | copy-start | bytes 24580
  90.0 13.3 %copy-start.9 = (f32[6,768]{1,0:T(8,128)S(1)}, f32[6,768]{1,0:T(8,128)}, u32[]{:S(2)}) copy-start(f32[6,768]{1,0:T(8,128)} %param.19) | copy-start | bytes 55300
  103.3 49.2 %copy-start.17 = (f32[768]{0:T(1024)}, f32[768]{0:T(1024)S(1)}, u32[]{:S(2)}) copy-start(f32[768]{0:T(1024)S(1)} %get-tuple-element.40) | copy-start | bytes 9220
  103.3 49.2 %copy-start.22 = (f32[768]{0:T(1024)}, f32[768]{0:T(1024)S(1)}, u32[]{:S(2)}) copy-start(f32[768]{0:T(1024)S(1)} %get-tuple-element.39) | copy-start | bytes 9220
  139.8 12.7 %copy-start.1 = (f32[1024,768]{1,0:T(8,128)}, f32[1024,768]{1,0:T(8,128)S(1)}, u32[]{:S(2)}) copy-start(f32[1024,768]{1,0:T(8,128)S(1)} %get-tuple-element.73) | copy-start | bytes 9437188
  139.9 12.7 %copy-start.11 = (f32[1024]{0:T(1024)}, f32[1024]{0:T(1024)S(1)}, u32[]{:S(2)}) copy-start(f32[1024]{0:T(1024)S(1)} %broadcast_multiply_fusion.4) | copy-start | bytes 12292
  140.4 12.2 %copy-start.15 = (f32[1024]{0:T(1024)}, f32[1024]{0:T(1024)S(1)}, u32[]{:S(2)}) copy-start(f32[1024]{0:T(1024)S(1)} %add_rsqrt_fusion.1) | copy-start | bytes 12292
  140.4 12.1 %copy-start.19 = (f32[3072]{0:T(1024)}, f32[3072]{0:T(1024)S(1)}, u32[]{:S(2)}) copy-start(f32[3072]{0:T(1024)S(1)} %add.192) | copy-start | bytes 36868
  152.5 11.0 %copy-start.31 = (bf16[1024,3072]{1,0:T(8,128)(2,1)}, bf16[1024,3072]{1,0:T(8,128)(2,1)S(1)}, u32[]{:S(2)}) copy-start(bf16[1024,3072]{1,0:T(8,128)(2,1)S(1)} %get-tuple-element.74) | copy-start | bytes 18874372
  165.8 10.9 %copy-start.30 = (s32[128,2]{0,1:T(2,128)S(1)}, s32[128,2]{0,1:T(2,128)}, u32[]{:S(2)}) copy-start(s32[128,2]{0,1:T(2,128)} %param.14) | copy-start | bytes 3076
  170.9 15.0 %all-to-all-start = ((bf16[16,8,768]{2,1,0:T(8,128)(2,1)}), bf16[16,8,768]{2,1,0:T(8,128)(2,1)S(1)}, u32[]{:S(2)}, u32[]{:S(2)}) async-start(bf16[16,8,768]{2,1,0:T(8,128)(2,1)} %fusion.9), calls=%async_computation | async-start | bytes 393216 | tf_op jit(solution)/shard_map/all_to_all | solution.py:835
  196.2 11.6 %all-to-all-start.1 = ((bf16[16,8,768]{2,1,0:T(8,128)(2,1)}), bf16[16,8,768]{2,1,0:T(8,128)(2,1)S(1)}, u32[]{:S(2)}, u32[]{:S(2)}) async-start(bf16[16,8,768]{2,1,0:T(8,128)(2,1)} %fusion.10), calls=%async_computation.1 | async-start | bytes 393216 | tf_op jit(solution)/shard_map/all_to_all | solution.py:846
  199.8 267.5 %all-gather.3.cloned.1.call-start = ((), (), s32[]{:S(2)}) async-start(), calls=%async_computation.2 | async-start | bytes 4718592 | tf_op jit(solution)/shard_map/all_gather | solution.py:814
  200.5 268.3 %all-gather.5.cloned.1.call-start = ((), (), s32[]{:S(2)}) async-start(), calls=%async_computation.3 | async-start | bytes 9437184 | tf_op jit(solution)/shard_map/all_gather | solution.py:878
  214.4 20.4 %slice-start = ((s8[4718592]{0:T(1024)(128)(4,1)}), s8[4194304]{0:T(1024)(128)(4,1)S(1)}, s32[]{:S(2)}) async-start(s8[4718592]{0:T(1024)(128)(4,1)} %bitcast.85), calls=%async_computation.4 | async-start | bytes 8388608
  221.6 13.3 %copy-start.2 = (f32[1024,768]{1,0:T(8,128)S(1)}, f32[1024,768]{1,0:T(8,128)}, u32[]{:S(2)}) copy-start(f32[1024,768]{1,0:T(8,128)} %copy-done.1) | copy-start | bytes 9437188
  221.6 13.3 %copy-start.12 = (f32[1024]{0:T(1024)S(1)}, f32[1024]{0:T(1024)}, u32[]{:S(2)}) copy-start(f32[1024]{0:T(1024)} %copy-done.11) | copy-start | bytes 12292
  221.6 13.2 %copy-start.16 = (f32[1024]{0:T(1024)S(1)}, f32[1024]{0:T(1024)}, u32[]{:S(2)}) copy-start(f32[1024]{0:T(1024)} %copy-done.15) | copy-start | bytes 12292
  221.6 13.2 %copy-start.18 = (f32[768]{0:T(1024)S(1)}, f32[768]{0:T(1024)}, u32[]{:S(2)}) copy-start(f32[768]{0:T(1024)} %copy-done.17) | copy-start | bytes 9220
  221.6 13.2 %slice-start.1 = ((s8[4718592]{0:T(1024)(128)(4,1)}), s8[524288]{0:T(1024)(128)(4,1)S(1)}, s32[]{:S(2)}) async-start(s8[4718592]{0:T(1024)(128)(4,1)} %bitcast.85), calls=%async_computation.5 | async-start | bytes 1048576
  387.5 63.1 %copy-start.3 = (f32[1744,128]{1,0:T(8,128)S(1)}, f32[1744,128]{1,0:T(8,128)}, u32[]{:S(2)}) copy-start(f32[1744,128]{1,0:T(8,128)} %scatter_lines.1) | copy-start | bytes 2678788
  453.0 13.6 %copy-start.10 = (f32[6,768]{1,0:T(8,128)S(1)}, f32[6,768]{1,0:T(8,128)}, u32[]{:S(2)}) copy-start(f32[6,768]{1,0:T(8,128)} %param.19) | copy-start | bytes 55300
  453.0 13.6 %copy-start.13 = (f32[6,768]{1,0:T(8,128)S(1)}, f32[6,768]{1,0:T(8,128)}, u32[]{:S(2)}) copy-start(f32[6,768]{1,0:T(8,128)} %param.20) | copy-start | bytes 55300
  453.0 13.6 %copy-start.14 = (f32[6,768]{1,0:T(8,128)S(1)}, f32[6,768]{1,0:T(8,128)}, u32[]{:S(2)}) copy-start(f32[6,768]{1,0:T(8,128)} %param.21) | copy-start | bytes 55300
  (18 other events, 84.0 us)
Sparse Core Ops, SparseCore 0:
  202.1 13.3 all-gather.2
  452.0 16.7 all-gather.4
